TPU v7x, 32 devices: a whole 2x2x4 slice. The times are simulated.
32 devices in a mesh: leaf: 2 (over y), user: 4 (over x, core), tensor: 4 (over z).
Axes of the slice: x: 2, y: 2, z: 4, core: 2. Of those that a mesh axis runs over, the one named last changes fastest.
Arguments:
- user_feat: bfloat16 [32, 128], P('user'), may hold values from -6 to 6
- beam_nodes: int32 [32, 128], P('user', ('leaf', 'tensor')), may hold values from 0 to 16383, as said below
- item_ids: int32 [32, 384], P('user', 'leaf'), may hold values from 0 to 16383, as said below
- subtree_slot: int32 [32], replicated, may hold values from 0 to 31, as said below
- node_table: bfloat16 [16384, 128], P(('leaf', 'tensor')), may hold values from -6 to 6
- item_table: bfloat16 [16384, 128], P(('leaf', 'tensor')), may hold values from -6 to 6
- mlp_user: bfloat16 [128, 1024], replicated, may hold values from -0.375 to 0.375
- mlp_node: bfloat16 [128, 1024], replicated, may hold values from -0.375 to 0.375
- mlp_bias: float32 [1024], replicated, may hold values from -3 to 3
- mlp_out: bfloat16 [1024], replicated, may hold values from -0.1875 to 0.1875
- proj_in: bfloat16 [384, 2048], P(None, 'tensor'), may hold values from -0.3125 to 0.3125
- cross_w: bfloat16 [2, 2048, 2048], P(None, None, 'tensor'), may hold values from -0.125 to 0.125
- cross_b: float32 [2, 2048], P(None, 'tensor'), may hold values from -3 to 3
- out_w: bfloat16 [2048], P('tensor'), may hold values from -0.125 to 0.125
Outputs:
- beam_score: float32 [32, 128], P('user', ('leaf', 'tensor'))
- interest: float32 [32, 128], P('user')
- logit: float32 [32, 384], P('user', 'leaf')
Inputs may be any that keep to these rules, and one draw needn't show every extreme that they name: A permutation of the subtrees: subtree s is held by index subtree_slot[s] // 4 of leaf+tensor (leaf-major), as its block subtree_slot[s] % 4. `beam_nodes`: within the 8 x 16 block of one device, at most 16 nodes belong to subtrees held by any one index of leaf+tensor; some index receives exactly 16 from every device's block. `item_ids`: split a device's 8 x 192 block, flattened user by user, into 4 runs of 384 items; each run has at most 48 items of subtrees held by any one index of leaf+tensor, and some index receives exactly 48 from every run.
All inputs are finite; a program needn't handle non-finite values.
Results may differ from a plain program's by a relative error of at most 0.0062.
Values may be sent and summed in bfloat16 or wider, within the bound.
A program may use at most 64 MiB of HBM per device.

v0:
```python
import math
import jax
import jax.numpy as jnp
from jax import lax
from jax.sharding import PartitionSpec as P

LAYERS = 2
SUB_NODES = 512
SUB_ITEMS = 512


def small_lookup(table, index):
    hits = index[:, None] == jnp.arange(table.shape[0], dtype=jnp.int32)[None, :]
    return jnp.sum(jnp.where(hits, table[None, :], 0), axis=1)


def bucket_slots(owner, owners, capacity):
    marks = (owner[:, None] == jnp.arange(owners, dtype=jnp.int32)[None, :]).astype(jnp.int32)
    before = jnp.cumsum(marks, axis=0) - marks
    rank = jnp.sum(before * marks, axis=1)
    return owner * capacity + rank


def place_ids(values, dest, total):
    return jnp.full((total,), -1, jnp.int32).at[dest].set(values)


def table_rows(table, wanted):
    found = table[jnp.clip(wanted, 0, None)]
    return jnp.where((wanted >= 0)[..., None], found, jnp.zeros_like(found))


def node_scores(user_rows, node_rows, mlp_node, mlp_bias, mlp_out):
    pre = user_rows + jnp.dot(node_rows, mlp_node, preferred_element_type=jnp.float32) + mlp_bias
    hidden = jax.nn.silu(pre).astype(jnp.bfloat16)
    return jnp.dot(hidden, mlp_out, preferred_element_type=jnp.float32)


def fetch_items(wanted_ids, capacity, owners, subtree_slot, item_table):
    sub_count = item_table.shape[0] // SUB_ITEMS
    slot = small_lookup(subtree_slot, wanted_ids // SUB_ITEMS)
    owner = slot // sub_count
    local = slot % sub_count * SUB_ITEMS + wanted_ids % SUB_ITEMS
    dest = bucket_slots(owner, owners, capacity)
    send = place_ids(local, dest, owners * capacity).reshape(owners, capacity)
    arrived = lax.all_to_all(
        table_rows(
            item_table,
            lax.all_to_all(send, ("leaf", "tensor"), split_axis=0, concat_axis=0, tiled=True),
        ),
        ("leaf", "tensor"),
        split_axis=0,
        concat_axis=0,
        tiled=True,
    )
    return arrived.reshape(owners * capacity, -1)[dest]


def per_device(
    user_feat,
    beam_nodes,
    item_ids,
    subtree_slot,
    node_table,
    item_table,
    mlp_user,
    mlp_node,
    mlp_bias,
    mlp_out,
    proj_in,
    cross_w,
    cross_b,
    out_w,
):
    leaf_count = lax.axis_size("leaf")
    tensor_count = lax.axis_size("tensor")
    owners = leaf_count * tensor_count
    users_here, beam_here = beam_nodes.shape
    requests = users_here * beam_here
    beam_cap = max(2, -(-requests // owners))
    sub_count = node_table.shape[0] // SUB_NODES
    flat_nodes = beam_nodes.reshape(-1)
    node_slot = small_lookup(subtree_slot, flat_nodes // SUB_NODES)
    node_owner = node_slot // sub_count
    node_local = node_slot % sub_count * SUB_NODES + flat_nodes % SUB_NODES
    node_dest = bucket_slots(node_owner, owners, beam_cap)
    node_send = place_ids(node_local, node_dest, owners * beam_cap).reshape(owners, beam_cap)
    user_part = jnp.dot(user_feat, mlp_user, preferred_element_type=jnp.float32)
    request_user = jnp.arange(requests, dtype=jnp.int32) // beam_here
    arrived = lax.all_to_all(
        table_rows(
            node_table,
            lax.all_to_all(node_send, ("leaf", "tensor"), split_axis=0, concat_axis=0, tiled=True),
        ),
        ("leaf", "tensor"),
        split_axis=0,
        concat_axis=0,
        tiled=True,
    )
    node_rows = arrived.reshape(owners * beam_cap, -1)[node_dest]
    scores = node_scores(user_part[request_user], node_rows, mlp_node, mlp_bias, mlp_out)
    weighted = jax.nn.sigmoid(scores)[:, None] * node_rows.astype(jnp.float32)
    numerator = jnp.sum(weighted.reshape(users_here, beam_here, -1), axis=1)
    interest_total = lax.psum(numerator, ("leaf", "tensor"))
    interest = interest_total / math.sqrt(owners * beam_here)
    beam_score = scores.reshape(users_here, beam_here)
    items_here = item_ids.shape[1]
    rows = users_here * items_here
    fetch = rows // tensor_count
    item_cap = max(2, -(-fetch // owners))
    flat_items = item_ids.reshape(-1)
    start = lax.axis_index("tensor") * fetch
    rotated = jnp.roll(flat_items, -start)
    rotated_rows = fetch_items(rotated, tensor_count * item_cap, owners, subtree_slot, item_table)
    item_vec = jnp.roll(rotated_rows, start, axis=0)
    interest_b = interest.astype(jnp.bfloat16)
    user_cols = jnp.repeat(user_feat, items_here, axis=0)
    interest_cols = jnp.repeat(interest_b, items_here, axis=0)
    inputs = jnp.concatenate([user_cols, interest_cols, item_vec], axis=1)
    x_first = jnp.dot(inputs, proj_in, preferred_element_type=jnp.float32).astype(jnp.bfloat16)
    first_wide = x_first.astype(jnp.float32)
    x_now = x_first
    for layer in range(LAYERS):
        weight = cross_w[layer]
        mixed = jnp.dot(
            lax.all_gather(x_now, "tensor", axis=1, tiled=True),
            weight,
            preferred_element_type=jnp.float32,
        )
        x_now = (first_wide * (mixed + cross_b[layer]) + x_now.astype(jnp.float32)).astype(
            jnp.bfloat16
        )
    partial_logit = jnp.dot(x_now, out_w, preferred_element_type=jnp.float32)
    logit = lax.psum(partial_logit, "tensor").reshape(users_here, items_here)
    return (beam_score, interest, logit)


def solution(mesh):
    placed = (
        P("user", None),
        P("user", ("leaf", "tensor")),
        P("user", "leaf"),
        P(),
        P(("leaf", "tensor"), None),
        P(("leaf", "tensor"), None),
        P(),
        P(),
        P(),
        P(),
        P(None, "tensor"),
        P(None, None, "tensor"),
        P(None, "tensor"),
        P("tensor"),
    )
    return jax.shard_map(
        per_device,
        mesh=mesh,
        in_specs=placed,
        out_specs=(P("user", ("leaf", "tensor")), P("user", None), P("user", "leaf")),
        check_vma=False,
    )
```

profile of v0, /device:TPU:0, one launch (start us, length us, event | category | flops | bytes accessed | tf_op | source)
XLA Modules:
  0.0 349.3 jit_solution(13803340638671157353)
XLA Ops:
  7.2 0.9 reshape.317
  9.3 1.0 scatter_custom_fusion
  10.9 7.3 %all-to-all-start = ((s32[8,1,16]{2,1,0:T(1,128)}), s32[8,1,16]{2,1,0:T(1,128)S(1)}, u32[]{:S(2)}, u32[]{:S(2)}) async-start(s32[8,1,16]{2,1,0:T(1,128)} %bitcast.4), calls=%async_computation | async-start | bytes 8192 | tf_op jit(solution)/shard_map/all_to_all | solution.py:93
  18.2 0.8 reshape.322
  20.0 2.3 reduce-window.6
  23.0 1.1 fusion.51
  24.1 6.2 %scatter_custom_fusion.1 = s32[1536]{0:T(1024)S(1)} fusion(s32[1536]{0:T(1024)S(1)} %fusion.36, s32[1536]{0:T(1024)S(1)} %get-tuple-element.5, s32[]{:T(128)} %constant.148.clone.1), kind=kCustom, calls=%fused_computation.98 | custom fusion | bytes 6148 | tf_op jit(solution)/shard_map/scatter | solution.py:25
  31.7 0.8 gather_fusion
  32.5 6.1 %all-to-all-start.2 = ((s32[8,1,192]{2,1,0:T(1,128)}), s32[8,1,192]{2,1,0:T(1,128)S(1)}, u32[]{:S(2)}, u32[]{:S(2)}) async-start(s32[8,1,192]{2,1,0:T(1,128)} %all_to_all.21), calls=%async_computation.2 | async-start | bytes 16384 | tf_op jit(solution)/shard_map/all_to_all | solution.py:49
  40.1 5.0 %all-to-all-done.2 = s32[8,1,192]{2,1,0:T(1,128)S(1)} async-done(((s32[8,1,192]{2,1,0:T(1,128)}), s32[8,1,192]{2,1,0:T(1,128)S(1)}, u32[]{:S(2)}, u32[]{:S(2)}) %all-to-all-start.2) | async-done | bytes 6176 | tf_op jit(solution)/shard_map/all_to_all | solution.py:49
  45.2 3.3 all-to-all-start.1
  48.6 3.2 gather_fusion.3
  51.8 1.0 broadcast_select_fusion
  52.8 2.3 all-to-all-done.1
  55.2 3.6 %all-to-all-start.3 = ((bf16[8,192,128]{2,1,0:T(8,128)(2,1)}), bf16[8,192,128]{2,1,0:T(8,128)(2,1)S(1)}, u32[]{:S(2)}, u32[]{:S(2)}) async-start(bf16[8,192,128]{2,1,0:T(8,128)(2,1)} %broadcast_select_fusion), calls=%async_computation.3 | async-start | bytes 786432 | tf_op jit(solution)/shard_map/all_to_all | solution.py:46
  60.2 21.9 %psum.14 = f32[8,128]{1,0:T(8,128)S(1)} all-reduce(f32[8,128]{1,0:T(8,128)S(1)} %fusion.22), channel_id=1, replica_groups=mesh['leaf'=2,'user'=4,'tensor'=4] {'leaf','tensor'}, use_global_device_ids=true, to_apply=%region_5.6 | all-reduce | flops 1024 | bytes 8192 | tf_op jit(solution)/shard_map/psum | solution.py:104
  82.7 3.2 gather_fusion.4
  85.9 1.5 fusion.19
  87.6 2.1 convolution_convert_fusion
  90.0 112.5 %all-gather.3.cloned.1.call-done = bf16[1536,2048]{1,0:T(8,128)(2,1)} async-done(((bf16[1536,512]{1,0:T(8,128)(2,1)}), bf16[1536,2048]{1,0:T(8,128)(2,1)}) %all-gather.3.cloned.1.call-update) | async-done | bytes 6291472 | tf_op jit(solution)/shard_map/all_gather | solution.py:126
  202.5 8.8 %fusion.1 = bf16[1536,512]{1,0:T(8,128)(2,1)} fusion(bf16[1536,512]{1,0:T(8,128)(2,1)} %convolution_convert_fusion, bf16[1536,2048]{1,0:T(8,128)(2,1)} %all-gather.3.cloned.1.call-done, bf16[2,2048,512]{2,1,0:T(8,128)(2,1)} %param.25, f32[512]{0:T(512)S(1)} %bitcast.106), kind=kOutput, calls=%fused_computation.12 | convolution fusion | flops 3225157632 | bytes 11536384 | tf_op jit(solution)/shard_map/dot_general | solution.py:125
  212.0 113.0 %all-gather.5.cloned.1.call-done = bf16[1536,2048]{1,0:T(8,128)(2,1)} async-done(((bf16[1536,512]{1,0:T(8,128)(2,1)}), bf16[1536,2048]{1,0:T(8,128)(2,1)}) %all-gather.5.cloned.1.call-update) | async-done | bytes 6291472 | tf_op jit(solution)/shard_map/all_gather | solution.py:126
  325.0 8.0 %fusion.16 = f32[1536]{0:T(1024)S(1)} fusion(bf16[512,1]{0,1:T(2,128)(2,1)S(1)} %reshape.389, bf16[1536,512]{1,0:T(8,128)(2,1)} %fusion.1, bf16[1536,2048]{1,0:T(8,128)(2,1)} %all-gather.5.cloned.1.call-done, bf16[1536,512]{1,0:T(8,128)(2,1)S(1)} %copy-done.1, bf16[2,2048,512]{2,1,0:T(8,128)(2,1)} %param.25, f32[512]{0:T(512)S(1)} %bitcast.105), kind=kOutput, calls=%fused_computation.27 | convolution fusion | flops 3227516928 | bytes 11543552 | tf_op jit(solution)/shard_map/dot_general | solution.py:133
  333.1 9.3 %psum.15 = f32[8,192]{1,0:T(8,128)} all-reduce(f32[8,192]{1,0:T(8,128)S(1)} %reshape.325), channel_id=1, replica_groups=mesh['leaf'=2,'user'=4,'tensor'=4] {'tensor'}, use_global_device_ids=true, to_apply=%region_11.12 | all-reduce | flops 1536 | bytes 12288 | tf_op jit(solution)/shard_map/psum | solution.py:134
  (68 shorter events, 9.6 us)
Async XLA Ops:
  7.2 41.4 %copy-start = (bf16[2048,128]{1,0:T(8,128)(2,1)S(1)}, bf16[2048,128]{1,0:T(8,128)(2,1)}, u32[]{:S(2)}) copy-start(bf16[2048,128]{1,0:T(8,128)(2,1)} %param.19) | copy-start | bytes 1572868
  7.2 31.6 %copy-start.2 = (bf16[2048,128]{1,0:T(8,128)(2,1)S(1)}, bf16[2048,128]{1,0:T(8,128)(2,1)}, u32[]{:S(2)}) copy-start(bf16[2048,128]{1,0:T(8,128)(2,1)} %param.18) | copy-start | bytes 1572868
  10.9 21.5 %all-to-all-start = ((s32[8,1,16]{2,1,0:T(1,128)}), s32[8,1,16]{2,1,0:T(1,128)S(1)}, u32[]{:S(2)}, u32[]{:S(2)}) async-start(s32[8,1,16]{2,1,0:T(1,128)} %bitcast.4), calls=%async_computation | async-start | bytes 8192 | tf_op jit(solution)/shard_map/all_to_all | solution.py:93
  32.5 27.1 %copy-start.7 = (bf16[128,1024]{1,0:T(8,128)(2,1)S(1)}, bf16[128,1024]{1,0:T(8,128)(2,1)}, u32[]{:S(2)}) copy-start(bf16[128,1024]{1,0:T(8,128)(2,1)} %param.21) | copy-start | bytes 786436
  32.5 27.1 %copy-start.8 = (f32[1024]{0:T(1024)S(1)}, f32[1024]{0:T(1024)}, u32[]{:S(2)}) copy-start(f32[1024]{0:T(1024)} %param.22) | copy-start | bytes 12292
  32.5 12.7 %all-to-all-start.2 = ((s32[8,1,192]{2,1,0:T(1,128)}), s32[8,1,192]{2,1,0:T(1,128)S(1)}, u32[]{:S(2)}, u32[]{:S(2)}) async-start(s32[8,1,192]{2,1,0:T(1,128)} %all_to_all.21), calls=%async_computation.2 | async-start | bytes 16384 | tf_op jit(solution)/shard_map/all_to_all | solution.py:49
  45.2 10.0 %all-to-all-start.1 = ((bf16[8,16,128]{2,1,0:T(8,128)(2,1)}), bf16[8,16,128]{2,1,0:T(8,128)(2,1)S(1)}, u32[]{:S(2)}, u32[]{:S(2)}) async-start(bf16[8,16,128]{2,1,0:T(8,128)(2,1)} %broadcast_select_fusion.1), calls=%async_computation.1 | async-start | bytes 65536 | tf_op jit(solution)/shard_map/all_to_all | solution.py:90
  55.2 27.5 %all-to-all-start.3 = ((bf16[8,192,128]{2,1,0:T(8,128)(2,1)}), bf16[8,192,128]{2,1,0:T(8,128)(2,1)S(1)}, u32[]{:S(2)}, u32[]{:S(2)}) async-start(bf16[8,192,128]{2,1,0:T(8,128)(2,1)} %broadcast_select_fusion), calls=%async_computation.3 | async-start | bytes 786432 | tf_op jit(solution)/shard_map/all_to_all | solution.py:46
  58.8 143.7 %all-gather.3.cloned.1.call-start = ((), (), s32[]{:S(2)}) async-start(), calls=%async_computation.4 | async-start | bytes 7864320 | tf_op jit(solution)/shard_map/all_gather | solution.py:126
  59.6 27.9 %copy-start.3 = (bf16[8,128]{1,0:T(8,128)(2,1)S(1)}, bf16[8,128]{1,0:T(8,128)(2,1)}, u32[]{:S(2)}) copy-start(bf16[8,128]{1,0:T(8,128)(2,1)} %param.14) | copy-start | bytes 6148
  59.9 27.6 %copy-start.6 = (bf16[384,512]{1,0:T(8,128)(2,1)S(1)}, bf16[384,512]{1,0:T(8,128)(2,1)}, u32[]{:S(2)}) copy-start(bf16[384,512]{1,0:T(8,128)(2,1)} %param.24) | copy-start | bytes 1179652
  87.5 2.4 copy-start.4
  89.7 235.3 %all-gather.5.cloned.1.call-start = ((), (), s32[]{:S(2)}) async-start(), calls=%async_computation.5 | async-start | bytes 7864320 | tf_op jit(solution)/shard_map/all_gather | solution.py:126
  202.5 8.9 %copy-start.5 = (bf16[512]{0:T(512)(128)(2,1)S(1)}, bf16[512]{0:T(512)(128)(2,1)}, u32[]{:S(2)}) copy-start(bf16[512]{0:T(512)(128)(2,1)} %param.27) | copy-start | bytes 3076
  202.5 122.5 %copy-start.1 = (bf16[1536,512]{1,0:T(8,128)(2,1)S(1)}, bf16[1536,512]{1,0:T(8,128)(2,1)}, u32[]{:S(2)}) copy-start(bf16[1536,512]{1,0:T(8,128)(2,1)} %convolution_convert_fusion) | copy-start | bytes 4718596
Sparse Core Ops, SparseCore 0:
  89.8 112.5 all-gather.2
  211.4 113.4 all-gather.4
where the time goes:
time: 350 us; the launch traced here: 349 us
  waiting for transfers between devices  233 us (67%)
  blocking collectives  31.2 us (9%)
  local copies, waits for them, and re-layouts  20.9 us (6%)
  starting transfers between devices  20.6 us (6%)
  matrix products  20.5 us (6%)
  between operations  14.4 us (4%)
  other arithmetic  8.75 us (2%)
    all_gather x2, waiting for transfers between devices, per_device(): lax.all_gather(x_now, 'tensor', axis=1, tiled=True)  225 us
    psum x1, blocking collectives, per_device(): interest_total = lax.psum(numerator, ('leaf', 'tensor'))  21.9 us
    psum x1, blocking collectives, per_device(): logit = lax.psum(partial_logit, 'tensor').reshape(users_here, items_here)  9.35 us
    dot_general x1, matrix products, per_device(): jnp.dot(lax.all_gather(x_now, 'tensor', axis=1, tiled=True), weight, pref...  8.83 us
    dot_general x1, matrix products, per_device(): partial_logit = jnp.dot(x_now, out_w, preferred_element_type=jnp.float32)  8.02 us
    all_to_all x1, starting transfers between devices, per_device(): lax.all_to_all(node_send, ('leaf', 'tensor'), split_axis=0, concat_axis=0...  7.31 us
    scatter x2, local copies, waits for them, and re-layouts, place_ids(): return jnp.full((total,), -1, jnp.int32).at[dest].set(values)  7.16 us
  transfers between devices with their start and end apart: 6, of which 4 were waited for; matrix products, arithmetic and copies ran while one was open for 6% of the time, Pallas kernels for 0%

commit v1 on v0

--- a/solution.py
+++ b/solution.py
@@ -7,6 +7,19 @@
 LAYERS = 2
 SUB_NODES = 512
 SUB_ITEMS = 512
+
+
+def ring_gather(x, axis, dim):
+    size, index, rows = (lax.axis_size(axis), lax.axis_index(axis), x.shape[dim])
+    right = [(i, (i + 1) % size) for i in range(size)]
+    result = jnp.zeros((*x.shape[:dim], size * rows, *x.shape[dim + 1 :]), x.dtype)
+    current = x
+    for hop in range(size):
+        source = (index - hop) % size
+        result = lax.dynamic_update_slice_in_dim(result, current, source * rows, axis=dim)
+        if hop < size - 1:
+            current = lax.ppermute(current, axis, right)
+    return result
 
 
 def small_lookup(table, index):
@@ -122,11 +135,7 @@
     x_now = x_first
     for layer in range(LAYERS):
         weight = cross_w[layer]
-        mixed = jnp.dot(
-            lax.all_gather(x_now, "tensor", axis=1, tiled=True),
-            weight,
-            preferred_element_type=jnp.float32,
-        )
+        mixed = jnp.dot(ring_gather(x_now, "tensor", 1), weight, preferred_element_type=jnp.float32)
         x_now = (first_wide * (mixed + cross_b[layer]) + x_now.astype(jnp.float32)).astype(
             jnp.bfloat16
         )

time: 350 us -> 319 us (0.911)
  waiting for transfers between devices: 233 us -> 195 us
  local copies, waits for them, and re-layouts: 20.9 us -> 42.8 us
  between operations: 14.4 us -> 1 us
    all_gather x2 -> x0, waiting for transfers between devices: 225 us -> none  [per_device(): lax.all_gather(x_now, 'tensor', axis=1, tiled=True)]
    ppermute x0 -> x6, waiting for transfers between devices: none -> 187 us  [ring_gather(): current = lax.ppermute(current, axis, right)]
    dynamic_update_slice x0 -> x6, local copies, waits for them, and re-layouts: none -> 13.5 us  [ring_gather(): lax.dynamic_update_slice_in_dim(result, current, source * rows, axis=dim)]
    another operation x0 -> x2, local copies, waits for them, and re-layouts: none -> 7.44 us
  transfers between devices with their start and end apart: 6 -> 10, of which waited for: 4 -> 8; matrix products, arithmetic and copies ran while one was open for 6% -> 9% of each run, Pallas kernels for 0% -> 0%
where the time goes in v1:
time: 319 us; the launch traced here: 318 us
  waiting for transfers between devices  195 us (61%)
  local copies, waits for them, and re-layouts  42.8 us (13%)
  blocking collectives  31 us (10%)
  starting transfers between devices  20.4 us (6%)
  matrix products  19.6 us (6%)
  other arithmetic  8.76 us (3%)
    ppermute x6, waiting for transfers between devices, ring_gather(): current = lax.ppermute(current, axis, right)  187 us
    psum x1, blocking collectives, per_device(): interest_total = lax.psum(numerator, ('leaf', 'tensor'))  21.9 us
    dynamic_update_slice x6, local copies, waits for them, and re-layouts, ring_gather(): lax.dynamic_update_slice_in_dim(result, current, source * rows, axis=dim)  13.5 us
    psum x1, blocking collectives, per_device(): logit = lax.psum(partial_logit, 'tensor').reshape(users_here, items_here)  9.07 us
    dot_general x1, matrix products, per_device(): partial_logit = jnp.dot(x_now, out_w, preferred_element_type=jnp.float32)  8.35 us
    dot_general x1, matrix products, per_device(): jnp.dot(ring_gather(x_now, 'tensor', 1), weight, preferred_element_type=j...  7.6 us
    another operation x2, local copies, waits for them, and re-layouts  7.44 us
    all_to_all x1, starting transfers between devices, per_device(): lax.all_to_all(node_send, ('leaf', 'tensor'), split_axis=0, concat_axis=0...  7.31 us
  transfers between devices with their start and end apart: 10, of which 8 were waited for; matrix products, arithmetic and copies ran while one was open for 9% of the time, Pallas kernels for 0%

profile of v1, /device:TPU:0, one launch (start us, length us, event | category | flops | bytes accessed | tf_op | source)
XLA Modules:
  0.0 318.2 jit_solution(1009153295056977786)
XLA Ops:
  4.4 7.3 %all-to-all-start = ((s32[8,1,16]{2,1,0:T(1,128)}), s32[8,1,16]{2,1,0:T(1,128)S(1)}, u32[]{:S(2)}, u32[]{:S(2)}) async-start(s32[8,1,16]{2,1,0:T(1,128)} %bitcast.4), calls=%async_computation | async-start | bytes 8192 | tf_op jit(solution)/shard_map/all_to_all | solution.py:106
  17.6 6.2 %scatter_custom_fusion.1 = s32[1536]{0:T(1024)S(1)} fusion(s32[1536]{0:T(1024)S(1)} %fusion.36, s32[1536]{0:T(1024)S(1)} %get-tuple-element.5, s32[]{:T(128)} %constant.182.clone.1), kind=kCustom, calls=%fused_computation.98 | custom fusion | bytes 6148 | tf_op jit(solution)/shard_map/scatter | solution.py:38
  26.0 6.1 %all-to-all-start.2 = ((s32[8,1,192]{2,1,0:T(1,128)}), s32[8,1,192]{2,1,0:T(1,128)S(1)}, u32[]{:S(2)}, u32[]{:S(2)}) async-start(s32[8,1,192]{2,1,0:T(1,128)} %all_to_all.21), calls=%async_computation.2 | async-start | bytes 16384 | tf_op jit(solution)/shard_map/all_to_all | solution.py:62
  33.6 5.0 %all-to-all-done.2 = s32[8,1,192]{2,1,0:T(1,128)S(1)} async-done(((s32[8,1,192]{2,1,0:T(1,128)}), s32[8,1,192]{2,1,0:T(1,128)S(1)}, u32[]{:S(2)}, u32[]{:S(2)}) %all-to-all-start.2) | async-done | bytes 6176 | tf_op jit(solution)/shard_map/all_to_all | solution.py:62
  38.7 3.3 %all-to-all-start.1 = ((bf16[8,16,128]{2,1,0:T(8,128)(2,1)}), bf16[8,16,128]{2,1,0:T(8,128)(2,1)S(1)}, u32[]{:S(2)}, u32[]{:S(2)}) async-start(bf16[8,16,128]{2,1,0:T(8,128)(2,1)} %broadcast_select_fusion.1), calls=%async_computation.1 | async-start | bytes 65536 | tf_op jit(solution)/shard_map/all_to_all | solution.py:103
  42.1 3.2 %gather_fusion.3 = bf16[1536,128]{1,0:T(8,128)(2,1)S(1)} fusion(bf16[2048,128]{1,0:T(8,128)(2,1)S(1)} %copy-done, s32[2048]{0:T(1024)S(1)} %pad_clamp_fusion.1), kind=kCustom, calls=%fused_computation.3 | custom fusion | bytes 792576 | tf_op jit(solution)/shard_map/gather | solution.py:42
  48.7 3.6 %all-to-all-start.3 = ((bf16[8,192,128]{2,1,0:T(8,128)(2,1)}), bf16[8,192,128]{2,1,0:T(8,128)(2,1)S(1)}, u32[]{:S(2)}, u32[]{:S(2)}) async-start(bf16[8,192,128]{2,1,0:T(8,128)(2,1)} %broadcast_select_fusion), calls=%async_computation.3 | async-start | bytes 786432 | tf_op jit(solution)/shard_map/all_to_all | solution.py:59
  53.6 21.9 %psum.14 = f32[8,128]{1,0:T(8,128)S(1)} all-reduce(f32[8,128]{1,0:T(8,128)S(1)} %fusion.22), channel_id=1, replica_groups=mesh['leaf'=2,'user'=4,'tensor'=4] {'leaf','tensor'}, use_global_device_ids=true, to_apply=%region_5.6 | all-reduce | flops 1024 | bytes 8192 | tf_op jit(solution)/shard_map/psum | solution.py:117
  76.2 3.2 %gather_fusion.4 = bf16[1536,128]{1,0:T(8,128)(2,1)S(1)} fusion(bf16[1536,128]{1,0:T(8,128)(2,1)S(1)} %bitcast.98, s32[2048]{0:T(1024)S(1)} %pad_clamp_fusion), kind=kCustom, calls=%fused_computation.4 | custom fusion | bytes 792576 | tf_op jit(solution)/shard_map/gather | solution.py:69
  81.0 3.5 %broadcast.396.clone = bf16[1536,2048]{1,0:T(8,128)(2,1)} broadcast(bf16[]{:T(256)} %constant.191.clone.1), dimensions={} | broadcast | bytes 6291458 | tf_op jit(solution)/shard_map/broadcast.14
  86.7 34.6 %collective-permute-done = bf16[1536,512]{1,0:T(8,128)(2,1)S(1)} collective-permute-done((bf16[1536,512]{1,0:T(8,128)(2,1)S(1)}, bf16[1536,512]{1,0:T(8,128)(2,1)S(1)}, u32[]{:S(2)}, u32[]{:S(2)}) %collective-permute-start) | collective-permute-done | bytes 1572896 | tf_op jit(solution)/shard_map/ppermute | solution.py:21
  121.2 34.3 %collective-permute-done.1 = bf16[1536,512]{1,0:T(8,128)(2,1)} collective-permute-done((bf16[1536,512]{1,0:T(8,128)(2,1)S(1)}, bf16[1536,512]{1,0:T(8,128)(2,1)}, u32[]{:S(2)}, u32[]{:S(2)}) %collective-permute-start.1) | collective-permute-done | bytes 1572896 | tf_op jit(solution)/shard_map/ppermute | solution.py:21
  156.9 2.7 constant_dynamic-update-slice_fusion.4
  159.7 26.3 %collective-permute-done.2 = bf16[1536,512]{1,0:T(8,128)(2,1)} collective-permute-done((bf16[1536,512]{1,0:T(8,128)(2,1)}, bf16[1536,512]{1,0:T(8,128)(2,1)}, u32[]{:S(2)}, u32[]{:S(2)}) %collective-permute-start.2) | collective-permute-done | bytes 1572896 | tf_op jit(solution)/shard_map/ppermute | solution.py:21
  186.0 2.7 constant_dynamic-update-slice_fusion.3
  188.7 4.0 %broadcast.396 = bf16[1536,2048]{1,0:T(8,128)(2,1)} broadcast(bf16[]{:T(256)} %constant.191.clone.1), dimensions={} | broadcast | bytes 6291458 | tf_op jit(solution)/shard_map/broadcast.14
  193.6 7.6 %constant_dynamic-update-slice_fusion.2 = (bf16[1536,2048]{1,0:T(8,128)(2,1)}, bf16[1536,512]{1,0:T(8,128)(2,1)S(1)}) fusion(bf16[1536,2048]{1,0:T(8,128)(2,1)} %broadcast.396, s32[]{:T(128)S(6)} %select_n.216, f32[512]{0:T(512)S(1)} %bitcast.108, bf16[1536,2048]{1,0:T(8,128)(2,1)} %constant_dynamic-update-slice_fusion.3, ...), kind=kOutput, calls=%fused_computation.105 | convolution fusion | flops 3225157632 | bytes 13109252 | tf_op jit(solution)/shard_map/dot_general | solution.py:138
  201.2 34.6 %collective-permute-done.3 = bf16[1536,512]{1,0:T(8,128)(2,1)S(1)} collective-permute-done((bf16[1536,512]{1,0:T(8,128)(2,1)S(1)}, bf16[1536,512]{1,0:T(8,128)(2,1)S(1)}, u32[]{:S(2)}, u32[]{:S(2)}) %collective-permute-start.3) | collective-permute-done | bytes 1572896 | tf_op jit(solution)/shard_map/ppermute | solution.py:21
  235.8 34.3 %collective-permute-done.4 = bf16[1536,512]{1,0:T(8,128)(2,1)} collective-permute-done((bf16[1536,512]{1,0:T(8,128)(2,1)S(1)}, bf16[1536,512]{1,0:T(8,128)(2,1)}, u32[]{:S(2)}, u32[]{:S(2)}) %collective-permute-start.4) | collective-permute-done | bytes 1572896 | tf_op jit(solution)/shard_map/ppermute | solution.py:21
  272.1 2.8 constant_dynamic-update-slice_fusion
  274.9 23.1 %collective-permute-done.5 = bf16[1536,512]{1,0:T(8,128)(2,1)} collective-permute-done((bf16[1536,512]{1,0:T(8,128)(2,1)}, bf16[1536,512]{1,0:T(8,128)(2,1)}, u32[]{:S(2)}, u32[]{:S(2)}) %collective-permute-start.5) | collective-permute-done | bytes 1572896 | tf_op jit(solution)/shard_map/ppermute | solution.py:21
  298.0 2.7 constant_dynamic-update-slice_fusion.7
  300.7 8.3 %fusion.16 = f32[1536]{0:T(1024)S(1)} fusion(bf16[512,1]{0,1:T(2,128)(2,1)S(1)} %reshape.389, bf16[1536,512]{1,0:T(8,128)(2,1)} %copy-done.8, bf16[1536,2048]{1,0:T(8,128)(2,1)} %constant_dynamic-update-slice_fusion.7, bf16[1536,512]{1,0:T(8,128)(2,1)} %copy-done.6, bf16[2,2048,512]{2,1,0:T(8,128)(2,1)} %param.25, f32[512]{0:T(512)S(1)} %bitcast.107), kind=kOutput, calls=%fused_computation.27 | convolution fusion | flops 3227516928 | bytes 11543552 | tf_op jit(solution)/shard_map/dot_general | solution.py:142
  309.1 9.1 %psum.15 = f32[8,192]{1,0:T(8,128)} all-reduce(f32[8,192]{1,0:T(8,128)S(1)} %reshape.325), channel_id=1, replica_groups=mesh['leaf'=2,'user'=4,'tensor'=4] {'tensor'}, use_global_device_ids=true, to_apply=%region_11.12 | all-reduce | flops 1536 | bytes 12288 | tf_op jit(solution)/shard_map/psum | solution.py:143
  (88 shorter events, 26.7 us)
Async XLA Ops:
  0.6 41.5 %copy-start = (bf16[2048,128]{1,0:T(8,128)(2,1)S(1)}, bf16[2048,128]{1,0:T(8,128)(2,1)}, u32[]{:S(2)}) copy-start(bf16[2048,128]{1,0:T(8,128)(2,1)} %param.19) | copy-start | bytes 1572868
  0.6 31.6 %copy-start.1 = (bf16[2048,128]{1,0:T(8,128)(2,1)S(1)}, bf16[2048,128]{1,0:T(8,128)(2,1)}, u32[]{:S(2)}) copy-start(bf16[2048,128]{1,0:T(8,128)(2,1)} %param.18) | copy-start | bytes 1572868
  4.4 21.6 %all-to-all-start = ((s32[8,1,16]{2,1,0:T(1,128)}), s32[8,1,16]{2,1,0:T(1,128)S(1)}, u32[]{:S(2)}, u32[]{:S(2)}) async-start(s32[8,1,16]{2,1,0:T(1,128)} %bitcast.4), calls=%async_computation | async-start | bytes 8192 | tf_op jit(solution)/shard_map/all_to_all | solution.py:106
  25.9 27.0 %copy-start.10 = (bf16[128,1024]{1,0:T(8,128)(2,1)S(1)}, bf16[128,1024]{1,0:T(8,128)(2,1)}, u32[]{:S(2)}) copy-start(bf16[128,1024]{1,0:T(8,128)(2,1)} %param.21) | copy-start | bytes 786436
  26.0 27.0 %copy-start.11 = (f32[1024]{0:T(1024)S(1)}, f32[1024]{0:T(1024)}, u32[]{:S(2)}) copy-start(f32[1024]{0:T(1024)} %param.22) | copy-start | bytes 12292
  26.0 12.7 %all-to-all-start.2 = ((s32[8,1,192]{2,1,0:T(1,128)}), s32[8,1,192]{2,1,0:T(1,128)S(1)}, u32[]{:S(2)}, u32[]{:S(2)}) async-start(s32[8,1,192]{2,1,0:T(1,128)} %all_to_all.21), calls=%async_computation.2 | async-start | bytes 16384 | tf_op jit(solution)/shard_map/all_to_all | solution.py:62
  38.7 10.0 %all-to-all-start.1 = ((bf16[8,16,128]{2,1,0:T(8,128)(2,1)}), bf16[8,16,128]{2,1,0:T(8,128)(2,1)S(1)}, u32[]{:S(2)}, u32[]{:S(2)}) async-start(bf16[8,16,128]{2,1,0:T(8,128)(2,1)} %broadcast_select_fusion.1), calls=%async_computation.1 | async-start | bytes 65536 | tf_op jit(solution)/shard_map/all_to_all | solution.py:103
  48.7 27.5 %all-to-all-start.3 = ((bf16[8,192,128]{2,1,0:T(8,128)(2,1)}), bf16[8,192,128]{2,1,0:T(8,128)(2,1)S(1)}, u32[]{:S(2)}, u32[]{:S(2)}) async-start(bf16[8,192,128]{2,1,0:T(8,128)(2,1)} %broadcast_select_fusion), calls=%async_computation.3 | async-start | bytes 786432 | tf_op jit(solution)/shard_map/all_to_all | solution.py:59
  53.0 28.0 %copy-start.2 = (bf16[8,128]{1,0:T(8,128)(2,1)S(1)}, bf16[8,128]{1,0:T(8,128)(2,1)}, u32[]{:S(2)}) copy-start(bf16[8,128]{1,0:T(8,128)(2,1)} %param.14) | copy-start | bytes 6148
  81.0 3.5 %copy-start.9 = (bf16[384,512]{1,0:T(8,128)(2,1)S(1)}, bf16[384,512]{1,0:T(8,128)(2,1)}, u32[]{:S(2)}) copy-start(bf16[384,512]{1,0:T(8,128)(2,1)} %param.24) | copy-start | bytes 1179652
  84.5 71.1 %copy-start.3 = (f32[2,512]{1,0:T(2,128)S(1)}, f32[2,512]{1,0:T(2,128)}, u32[]{:S(2)}) copy-start(f32[2,512]{1,0:T(2,128)} %param.26) | copy-start | bytes 12292
  86.7 68.9 %copy-start.6 = (bf16[1536,512]{1,0:T(8,128)(2,1)}, bf16[1536,512]{1,0:T(8,128)(2,1)S(1)}, u32[]{:S(2)}) copy-start(bf16[1536,512]{1,0:T(8,128)(2,1)S(1)} %get-tuple-element.14) | copy-start | bytes 4718596
  86.7 34.6 %collective-permute-start = (bf16[1536,512]{1,0:T(8,128)(2,1)S(1)}, bf16[1536,512]{1,0:T(8,128)(2,1)S(1)}, u32[]{:S(2)}, u32[]{:S(2)}) collective-permute-start(bf16[1536,512]{1,0:T(8,128)(2,1)S(1)} %get-tuple-element.14), channel_id=1, source_target_pairs={{0,1},{1,2},{2,3},{3,0},{4,5},{5,6},{6,7},{7,4},{8,9},{9,10},{10,1... | collective-permute-start | bytes 4718600 | tf_op jit(solution)/shard_map/ppermute | solution.py:21
  121.2 34.3 %collective-permute-start.1 = (bf16[1536,512]{1,0:T(8,128)(2,1)S(1)}, bf16[1536,512]{1,0:T(8,128)(2,1)}, u32[]{:S(2)}, u32[]{:S(2)}) collective-permute-start(bf16[1536,512]{1,0:T(8,128)(2,1)S(1)} %collective-permute-done), channel_id=1, source_target_pairs={{0,1},{1,2},{2,3},{3,0},{4,5},{5,6},{6,7},{7,4},{8,9},{9,10},{10,1... | collective-permute-start | bytes 4718600 | tf_op jit(solution)/shard_map/ppermute | solution.py:21
  155.6 30.4 %collective-permute-start.2 = (bf16[1536,512]{1,0:T(8,128)(2,1)}, bf16[1536,512]{1,0:T(8,128)(2,1)}, u32[]{:S(2)}, u32[]{:S(2)}) collective-permute-start(bf16[1536,512]{1,0:T(8,128)(2,1)} %collective-permute-done.1), channel_id=1, source_target_pairs={{0,1},{1,2},{2,3},{3,0},{4,5},{5,6},{6,7},{7,4},{8,9},{9,10},{10,1... | collective-permute-start | bytes 4718600 | tf_op jit(solution)/shard_map/ppermute | solution.py:21
  188.7 4.0 %copy-start.5 = (bf16[2,2048,512]{2,1,0:T(8,128)(2,1)S(1)}, bf16[2,2048,512]{2,1,0:T(8,128)(2,1)}, u32[]{:S(2)}) copy-start(bf16[2,2048,512]{2,1,0:T(8,128)(2,1)} %param.25) | copy-start | bytes 12582916
  188.7 4.9 %copy-start.7 = (bf16[1536,512]{1,0:T(8,128)(2,1)S(1)}, bf16[1536,512]{1,0:T(8,128)(2,1)}, u32[]{:S(2)}) copy-start(bf16[1536,512]{1,0:T(8,128)(2,1)} %copy-done.6) | copy-start | bytes 4718596
  193.6 76.5 %copy-start.4 = (bf16[512]{0:T(512)(128)(2,1)S(1)}, bf16[512]{0:T(512)(128)(2,1)}, u32[]{:S(2)}) copy-start(bf16[512]{0:T(512)(128)(2,1)} %param.27) | copy-start | bytes 3076
  201.2 68.9 %copy-start.8 = (bf16[1536,512]{1,0:T(8,128)(2,1)}, bf16[1536,512]{1,0:T(8,128)(2,1)S(1)}, u32[]{:S(2)}) copy-start(bf16[1536,512]{1,0:T(8,128)(2,1)S(1)} %get-tuple-element.16) | copy-start | bytes 4718596
  201.2 34.6 %collective-permute-start.3 = (bf16[1536,512]{1,0:T(8,128)(2,1)S(1)}, bf16[1536,512]{1,0:T(8,128)(2,1)S(1)}, u32[]{:S(2)}, u32[]{:S(2)}) collective-permute-start(bf16[1536,512]{1,0:T(8,128)(2,1)S(1)} %get-tuple-element.16), channel_id=1, source_target_pairs={{0,1},{1,2},{2,3},{3,0},{4,5},{5,6},{6,7},{7,4},{8,9},{9,10},{10,1... | collective-permute-start | bytes 4718600 | tf_op jit(solution)/shard_map/ppermute | solution.py:21
  235.8 34.3 %collective-permute-start.4 = (bf16[1536,512]{1,0:T(8,128)(2,1)S(1)}, bf16[1536,512]{1,0:T(8,128)(2,1)}, u32[]{:S(2)}, u32[]{:S(2)}) collective-permute-start(bf16[1536,512]{1,0:T(8,128)(2,1)S(1)} %collective-permute-done.3), channel_id=1, source_target_pairs={{0,1},{1,2},{2,3},{3,0},{4,5},{5,6},{6,7},{7,4},{8,9},{9,10},{10,1... | collective-permute-start | bytes 4718600 | tf_op jit(solution)/shard_map/ppermute | solution.py:21
  270.1 27.9 %collective-permute-start.5 = (bf16[1536,512]{1,0:T(8,128)(2,1)}, bf16[1536,512]{1,0:T(8,128)(2,1)}, u32[]{:S(2)}, u32[]{:S(2)}) collective-permute-start(bf16[1536,512]{1,0:T(8,128)(2,1)} %collective-permute-done.4), channel_id=1, source_target_pairs={{0,1},{1,2},{2,3},{3,0},{4,5},{5,6},{6,7},{7,4},{8,9},{9,10},{10,1... | collective-permute-start | bytes 4718600 | tf_op jit(solution)/shard_map/ppermute | solution.py:21
